TPU v7x, 32 devices: a whole 2x2x4 slice. The times are simulated.
32 devices in a mesh: seq: 8 (over z, y), mp: 4 (over x, core).
Axes of the slice: x: 2, y: 2, z: 4, core: 2. Of those that a mesh axis runs over, the one named last changes fastest.
Arguments:
- block_input: bfloat16 [1, 1280, 2560], P(None, 'seq'), may hold values from -6 to 6
- mix_gain: float32 [2560], replicated, may hold values from 0.5 to 1.5
- x_weight: bfloat16 [2560, 2560], P(None, 'mp'), may hold values from -0.125 to 0.125
- y_weight: bfloat16 [2560, 2560], P(None, 'mp'), may hold values from -0.125 to 0.125
- conv_weight: float32 [4, 2560], P(None, 'mp'), may hold values from -3 to 3
- conv_bias: float32 [2560], P('mp'), may hold values from -3 to 3
- input_gate: bfloat16 [256, 2560], P(None, 'mp'), may hold values from -0.375 to 0.375
- decay_gate: bfloat16 [256, 2560], P(None, 'mp'), may hold values from -0.375 to 0.375
- decay_param: float32 [2560], P('mp'), may hold values from -13 to -5
- out_weight: bfloat16 [2560, 2560], P('mp'), may hold values from -0.125 to 0.125
- ffn_gain: float32 [2560], replicated, may hold values from 0.5 to 1.5
- gate_weight: bfloat16 [2560, 7680], P(None, 'mp'), may hold values from -0.125 to 0.125
- up_weight: bfloat16 [2560, 7680], P(None, 'mp'), may hold values from -0.125 to 0.125
- down_weight: bfloat16 [7680, 2560], P('mp'), may hold values from -0.0625 to 0.0625
- out_cotangent: bfloat16 [1, 1280, 2560], P(None, 'seq'), may hold values from -6 to 6
Outputs:
- block_output: bfloat16 [1, 1280, 2560], P(None, 'seq')
- input_grad: bfloat16 [1, 1280, 2560], P(None, 'seq')
- mix_gain_grad: float32 [2560], P('seq')
- x_weight_grad: float32 [2560, 2560], P('seq', 'mp')
- y_weight_grad: float32 [2560, 2560], P('seq', 'mp')
- conv_weight_grad: float32 [4, 2560], P(None, ('mp', 'seq'))
- conv_bias_grad: float32 [2560], P(('mp', 'seq'))
- input_gate_grad: float32 [256, 2560], P('seq', 'mp')
- decay_gate_grad: float32 [256, 2560], P('seq', 'mp')
- decay_param_grad: float32 [2560], P(('mp', 'seq'))
- out_weight_grad: float32 [2560, 2560], P('mp', 'seq')
- ffn_gain_grad: float32 [2560], P('seq')
- gate_weight_grad: float32 [2560, 7680], P('seq', 'mp')
- up_weight_grad: float32 [2560, 7680], P('seq', 'mp')
- down_weight_grad: float32 [7680, 2560], P('mp', 'seq')
All inputs are finite; a program needn't handle non-finite values.
Results may differ from a plain program's by a relative error of at most 0.009.
Values may be sent and summed in bfloat16 or wider, within the bound.
No kernel may reach another device: no remote copies, remote signals or barrier semaphores. Data moves between devices by JAX's collectives and lax.ppermute only.
A program may use at most 320 MiB of HBM per device.

v0:
```python
import jax
import jax.numpy as jnp
from jax import lax
from jax.sharding import PartitionSpec as P

EPS = 1e-06


def passed_along(shard, axis, by):
    size = lax.axis_size(axis)
    pairs = [(i, i + by) for i in range(size) if 0 <= i + by < size]
    return lax.ppermute(shard, axis, pairs)


def carried_in(value, axis, join, neutral, backward):
    count, mine = (lax.axis_size(axis), lax.axis_index(axis))
    pieces = jax.tree.map(lambda part: lax.all_gather(part, axis), value)
    if backward:
        pieces = jax.tree.map(lambda part: part[::-1], pieces)
        mine = count - 1 - mine
    so_far = jax.tree.map(
        lambda part, zero: jnp.full_like(part, 0) + jnp.asarray(zero, part.dtype), value, neutral
    )

    def lap(position, so_far):
        longer = join(so_far, jax.tree.map(lambda part: part[position], pieces))
        return jax.tree.map(lambda new, old: jnp.where(position < mine, new, old), longer, so_far)

    return lax.fori_loop(0, count - 1, lap, so_far)


def gelu_tanh(values):
    return jax.nn.gelu(values, approximate=True)


def gelu_slope(values):
    _, pullback = jax.vjp(gelu_tanh, values)
    return pullback(jnp.ones_like(values))[0]


def bdot(left, right):
    return jnp.dot(left, right, preferred_element_type=jnp.float32)


def link_pairs(earlier, later):
    return (earlier[0] * later[0], later[0] * earlier[1] + later[1])


def per_device(
    block_input,
    mix_gain,
    x_weight,
    y_weight,
    conv_weight,
    conv_bias,
    input_gate,
    decay_gate,
    decay_param,
    out_weight,
    ffn_gain,
    gate_weight,
    up_weight,
    down_weight,
    out_cotangent,
):
    seq_count, group_len, model_width = block_input.shape
    local_w = x_weight.shape[1]
    head_size = input_gate.shape[0]
    full_w = local_w * lax.axis_size("mp")
    row_count = seq_count * group_len
    owner = lax.axis_index("mp")
    row_heads = jnp.arange(full_w, dtype=jnp.int32) // head_size
    col_heads = (owner * local_w + jnp.arange(local_w, dtype=jnp.int32)) // head_size
    head_mask = row_heads[:, None] == col_heads[None, :]
    dense_x = jnp.where(
        head_mask, jnp.tile(input_gate, (full_w // head_size, 1)), jnp.zeros((), jnp.bfloat16)
    )
    dense_a = jnp.where(
        head_mask, jnp.tile(decay_gate, (full_w // head_size, 1)), jnp.zeros((), jnp.bfloat16)
    )
    inp = block_input.reshape(row_count, model_width).astype(jnp.float32)
    r_one = lax.rsqrt(jnp.mean(inp * inp, axis=-1, keepdims=True) + EPS)
    n_one = inp * r_one
    normed1 = (n_one * mix_gain).astype(jnp.bfloat16)
    x_branch = bdot(normed1, x_weight)
    y_branch = bdot(normed1, y_weight)
    y_gated = gelu_tanh(y_branch)
    x_three = x_branch.reshape(seq_count, group_len, local_w)
    before = passed_along(x_three[:, group_len - 3 :, :], "seq", 1)
    padded = jnp.concatenate([before, x_three], axis=1)
    conv_three = conv_bias + sum(
        (conv_weight[offset] * padded[:, offset : offset + group_len] for offset in range(4))
    )
    conv_out = conv_three.reshape(row_count, local_w)
    conv_low = conv_out.astype(jnp.bfloat16)
    gathered = lax.all_gather(conv_low, "mp", axis=1, tiled=True)
    gate_x = jax.nn.sigmoid(bdot(gathered, dense_x))
    gate_a = jax.nn.sigmoid(bdot(gathered, dense_a))
    softer = jax.nn.softplus(decay_param)
    log_decay = -8.0 * softer * gate_a
    decay = jnp.exp(log_decay)
    mult = jnp.sqrt(-jnp.expm1(2.0 * log_decay))
    drive = conv_out * gate_x * mult
    decay_three = decay.reshape(seq_count, group_len, local_w)
    prod_three, local_state = lax.associative_scan(
        link_pairs, (decay_three, drive.reshape(seq_count, group_len, local_w)), axis=1
    )
    block_prod = prod_three[:, -1]
    ones_init = jnp.ones((seq_count, local_w), jnp.float32)
    zero_init = jnp.zeros((seq_count, local_w), jnp.float32)
    carried = carried_in(
        (block_prod, local_state[:, -1]), "seq", link_pairs, (ones_init, zero_init), False
    )
    state_in = carried[1]
    hidden_three = local_state + prod_three * state_in[:, None, :]
    hidden = hidden_three.reshape(row_count, local_w)
    mixed = (hidden * y_gated).astype(jnp.bfloat16)
    x_one = inp + lax.psum(bdot(mixed, out_weight), "mp")
    r_two = lax.rsqrt(jnp.mean(x_one * x_one, axis=-1, keepdims=True) + EPS)
    n_two = x_one * r_two
    normed2 = (n_two * ffn_gain).astype(jnp.bfloat16)
    gate_pre = bdot(normed2, gate_weight)
    up_pre = bdot(normed2, up_weight)
    act = (gelu_tanh(gate_pre) * up_pre).astype(jnp.bfloat16)
    ffn_out = lax.psum(bdot(act, down_weight), "mp")
    block_output = (x_one + ffn_out).astype(jnp.bfloat16).reshape(seq_count, group_len, model_width)
    cot_low = out_cotangent.reshape(row_count, model_width)
    cot = cot_low.astype(jnp.float32)
    d_act = bdot(cot_low, down_weight.T)
    g_down = bdot(act.T, cot_low)
    d_gate = (d_act * up_pre * gelu_slope(gate_pre)).astype(jnp.bfloat16)
    d_up = (d_act * gelu_tanh(gate_pre)).astype(jnp.bfloat16)
    g_gate = bdot(normed2.T, d_gate)
    g_up = bdot(normed2.T, d_up)
    d_n_two = lax.psum(bdot(d_gate, gate_weight.T) + bdot(d_up, up_weight.T), "mp")
    g_ffn_gain = jnp.sum(d_n_two * n_two, axis=0)
    e_two = ffn_gain * d_n_two
    d_x_one = cot + r_two * (e_two - n_two * jnp.mean(e_two * n_two, axis=-1, keepdims=True))
    d_x_low = d_x_one.astype(jnp.bfloat16)
    g_out = bdot(mixed.T, d_x_low)
    d_mixed = bdot(d_x_low, out_weight.T)
    d_y_low = (d_mixed * hidden * gelu_slope(y_branch)).astype(jnp.bfloat16)
    direct = (d_mixed * y_gated).reshape(seq_count, group_len, local_w)
    decay_next = jnp.concatenate(
        [decay_three[:, 1:], jnp.ones((seq_count, 1, local_w), jnp.float32)], axis=1
    )
    after_prod, local_lam = lax.associative_scan(
        link_pairs, (decay_next, direct), reverse=True, axis=1
    )
    first_term = decay_three[:, 0] * local_lam[:, 0]
    returned = carried_in((block_prod, first_term), "seq", link_pairs, (ones_init, zero_init), True)
    lam = (local_lam + after_prod * returned[1][:, None, :]).reshape(row_count, local_w)
    hidden_prev = jnp.concatenate([state_in[:, None, :], hidden_three[:, :-1]], axis=1).reshape(
        row_count, local_w
    )
    d_log = lam * hidden_prev * decay - lam * conv_out * gate_x * decay * decay / mult
    g_decay = jnp.sum(d_log * (-8.0 * gate_a) * jax.nn.sigmoid(decay_param), axis=0)
    d_gx = (lam * conv_out * mult * gate_x * (1.0 - gate_x)).astype(jnp.bfloat16)
    d_ga = (d_log * (-8.0 * softer) * gate_a * (1.0 - gate_a)).astype(jnp.bfloat16)
    dense_gx = jnp.where(head_mask, bdot(gathered.T, d_gx), 0.0)
    dense_ga = jnp.where(head_mask, bdot(gathered.T, d_ga), 0.0)
    g_input_gate = jnp.sum(dense_gx.reshape(full_w // head_size, head_size, local_w), axis=0)
    g_decay_gate = jnp.sum(dense_ga.reshape(full_w // head_size, head_size, local_w), axis=0)
    back_terms = bdot(d_gx, dense_x.T) + bdot(d_ga, dense_a.T)
    back_own = lax.psum_scatter(back_terms, "mp", scatter_dimension=1, tiled=True)
    d_conv = lam * gate_x * mult + back_own
    g_conv_bias = jnp.sum(d_conv, axis=0)
    d_conv_three = d_conv.reshape(seq_count, group_len, local_w)
    g_conv = jnp.stack(
        [
            jnp.sum(d_conv_three * padded[:, offset : offset + group_len], axis=(0, 1))
            for offset in range(4)
        ]
    )
    later_rows = passed_along(d_conv_three[:, :3, :], "seq", -1)
    padded_back = jnp.concatenate([d_conv_three, later_rows], axis=1)
    d_x_three = sum(
        (
            conv_weight[offset] * padded_back[:, 3 - offset : 3 - offset + group_len]
            for offset in range(4)
        )
    )
    d_x_branch = d_x_three.reshape(row_count, local_w).astype(jnp.bfloat16)
    g_x = bdot(normed1.T, d_x_branch)
    g_y = bdot(normed1.T, d_y_low)
    d_n_one = lax.psum(bdot(d_x_branch, x_weight.T) + bdot(d_y_low, y_weight.T), "mp")
    g_mix_gain = jnp.sum(d_n_one * n_one, axis=0)
    e_one = mix_gain * d_n_one
    d_input = d_x_one + r_one * (e_one - n_one * jnp.mean(e_one * n_one, axis=-1, keepdims=True))
    input_grad = d_input.astype(jnp.bfloat16).reshape(seq_count, group_len, model_width)
    summed = (
        lax.psum_scatter(g_mix_gain, "seq", scatter_dimension=0, tiled=True),
        lax.psum_scatter(g_x, "seq", scatter_dimension=0, tiled=True),
        lax.psum_scatter(g_y, "seq", scatter_dimension=0, tiled=True),
        lax.psum_scatter(g_conv, "seq", scatter_dimension=1, tiled=True),
        lax.psum_scatter(g_conv_bias, "seq", scatter_dimension=0, tiled=True),
        lax.psum_scatter(g_input_gate, "seq", scatter_dimension=0, tiled=True),
        lax.psum_scatter(g_decay_gate, "seq", scatter_dimension=0, tiled=True),
        lax.psum_scatter(g_decay, "seq", scatter_dimension=0, tiled=True),
        lax.psum_scatter(g_out, "seq", scatter_dimension=1, tiled=True),
        lax.psum_scatter(g_ffn_gain, "seq", scatter_dimension=0, tiled=True),
        lax.psum_scatter(g_gate, "seq", scatter_dimension=0, tiled=True),
        lax.psum_scatter(g_up, "seq", scatter_dimension=0, tiled=True),
        lax.psum_scatter(g_down, "seq", scatter_dimension=1, tiled=True),
    )
    return (
        block_output,
        input_grad,
        summed[0],
        summed[1],
        summed[2],
        summed[3],
        summed[4],
        summed[5],
        summed[6],
        summed[7],
        summed[8],
        summed[9],
        summed[10],
        summed[11],
        summed[12],
    )


def solution(mesh):
    in_specs = (
        P(None, "seq", None),
        P(),
        P(None, "mp"),
        P(None, "mp"),
        P(None, "mp"),
        P("mp"),
        P(None, "mp"),
        P(None, "mp"),
        P("mp"),
        P("mp", None),
        P(),
        P(None, "mp"),
        P(None, "mp"),
        P("mp", None),
        P(None, "seq", None),
    )
    out_specs = (
        P(None, "seq", None),
        P(None, "seq", None),
        P("seq"),
        P("seq", "mp"),
        P("seq", "mp"),
        P(None, ("mp", "seq")),
        P(("mp", "seq")),
        P("seq", "mp"),
        P("seq", "mp"),
        P(("mp", "seq")),
        P("mp", "seq"),
        P("seq"),
        P("seq", "mp"),
        P("seq", "mp"),
        P("mp", "seq"),
    )
    return jax.shard_map(
        per_device, mesh=mesh, in_specs=in_specs, out_specs=out_specs, check_vma=False
    )
```

profile of v0, /device:TPU:0, one launch (start us, length us, event | category | flops | bytes accessed | tf_op | source)
XLA Modules:
  0.0 2168.8 jit_solution(16874175498636065759)
XLA Ops:
  12.6 4.9 collective-permute-start
  21.0 8.8 all_gather.14
  111.2 30.8 %all_gather.15 = f32[8,1,640]{2,1,0:T(1,128)S(1)} all-gather(f32[1,1,640]{2,1,0:T(1,128)S(1)} %slice_add_fusion.2), channel_id=1, replica_groups=mesh['seq'=8,'mp'=4] {'seq'}, dimensions={0}, use_global_device_ids=true | all-gather | bytes 23040 | tf_op jit(solution)/shard_map/all_gather | solution.py:17
  145.3 30.4 %all_gather.16 = f32[8,1,640]{2,1,0:T(1,128)S(1)} all-gather(f32[1,1,640]{2,1,0:T(1,128)S(1)} %slice_add_fusion.1), channel_id=1, replica_groups=mesh['seq'=8,'mp'=4] {'seq'}, dimensions={0}, use_global_device_ids=true | all-gather | bytes 23040 | tf_op jit(solution)/shard_map/all_gather | solution.py:17
  182.2 42.2 %all-reduce.68.cloned.1.call-done = f32[160,2560]{1,0:T(8,128)} async-done(((f32[160,2560]{1,0:T(8,128)}), f32[160,2560]{1,0:T(8,128)}) %all-reduce.68.cloned.1.call-update) | async-done | bytes 1638416 | tf_op jit(solution)/shard_map/psum | solution.py:118
  227.8 6.2 fusion.118
  236.5 8.1 multiply_convert_fusion.1
  247.9 8.3 convolution_add_fusion.2
  273.1 27.3 %all-reduce.70.cloned.1.call-done = f32[160,2560]{1,0:T(8,128)} async-done(((f32[160,2560]{1,0:T(8,128)}), f32[160,2560]{1,0:T(8,128)}) %all-reduce.70.cloned.1.call-update) | async-done | bytes 1638416 | tf_op jit(solution)/shard_map/psum | solution.py:135
  308.1 5.6 reverse.8
  440.6 5.6 rev.17
  446.2 30.5 %all_gather.17 = f32[8,1,640]{2,1,0:T(1,128)S(1)} all-gather(f32[1,1,640]{2,1,0:T(1,128)S(1)} %add_multiply_fusion.20), channel_id=1, replica_groups=mesh['seq'=8,'mp'=4] {'seq'}, dimensions={0}, use_global_device_ids=true | all-gather | bytes 23040 | tf_op jit(solution)/shard_map/all_gather | solution.py:17
  476.7 4.8 while.29
  488.4 5.6 rev.18
  502.8 7.1 fusion.119
  509.8 21.3 reduce-scatter.13.cloned.1.call-done
  553.0 4.2 reduce_sum.137
  560.9 4.2 reduce_sum.136
  575.3 4.1 fusion.33
  580.7 8.4 fusion.36
  590.4 8.2 fusion.123
  599.7 8.4 fusion.122
  612.1 60.4 %all-reduce.72.cloned.1.call-done = (f32[160,2560]{1,0:T(8,128)}, f32[160,2560]{1,0:T(8,128)}) async-done(((f32[160,2560]{1,0:T(8,128)}, f32[160,2560]{1,0:T(8,128)}), (f32[160,2560]{1,0:T(8,128)}, f32[160,2560]{1,0:T(8,128)})) %all-reduce.72.cloned.1.call-update) | async-done | bytes 3276816 | tf_op jit(solution)/shard_map/psum | solution.py:125
  674.5 37.3 %all-reduce.62 = (f32[2560]{0:T(1024)S(1)}, f32[640]{0:T(1024)S(1)}, f32[640]{0:T(1024)S(1)}, f32[2560]{0:T(1024)S(1)}) all-reduce(f32[2560]{0:T(1024)S(1)} %get-tuple-element.243, f32[640]{0:T(1024)S(1)} %get-tuple-element.248, f32[640]{0:T(1024)S(1)} %get-tuple-element.281, ...), channel_id=3, replica_groups=mesh['seq'=8,'mp'=4] {'seq'}, use_global_device_ids=true, to_apply=%region_14.15.clone | all-reduce | flops 6400 | bytes 51200
  718.9 20.2 reduce-scatter.21.cloned.1.call-done
  739.1 65.6 %reduce-scatter.19.cloned.1.call-done = f32[32,640]{1,0:T(8,128)} async-done(((f32[256,640]{1,0:T(8,128)}), f32[32,640]{1,0:T(8,128)}) %reduce-scatter.19.cloned.1.call-update) | async-done | bytes 81936 | tf_op jit(solution)/shard_map/reduce_scatter | solution.py:197
  804.7 125.0 %reduce-scatter.23.cloned.1.call-done = f32[640,320]{0,1:T(8,128)} async-done(((f32[640,2560]{0,1:T(8,128)}), f32[640,320]{0,1:T(8,128)}) %reduce-scatter.23.cloned.1.call-update) | async-done | bytes 819216 | tf_op jit(solution)/shard_map/reduce_scatter | solution.py:200
  929.8 125.2 %reduce-scatter.17.cloned.1.call-done = f32[320,640]{1,0:T(8,128)} async-done(((f32[2560,640]{1,0:T(8,128)}), f32[320,640]{1,0:T(8,128)}) %reduce-scatter.17.cloned.1.call-update) | async-done | bytes 819216 | tf_op jit(solution)/shard_map/reduce_scatter | solution.py:194
  1055.0 125.1 %reduce-scatter.15.cloned.1.call-done = f32[320,640]{1,0:T(8,128)} async-done(((f32[2560,640]{1,0:T(8,128)}), f32[320,640]{1,0:T(8,128)}) %reduce-scatter.15.cloned.1.call-update) | async-done | bytes 819216 | tf_op jit(solution)/shard_map/reduce_scatter | solution.py:193
  1180.1 327.6 %reduce-scatter.29.cloned.1.call-done = f32[1920,320]{0,1:T(8,128)} async-done(((f32[1920,2560]{0,1:T(8,128)}), f32[1920,320]{0,1:T(8,128)}) %reduce-scatter.29.cloned.1.call-update) | async-done | bytes 2457616 | tf_op jit(solution)/shard_map/reduce_scatter | solution.py:204
  1507.6 327.2 %reduce-scatter.27.cloned.1.call-done = f32[320,1920]{1,0:T(8,128)} async-done(((f32[2560,1920]{1,0:T(8,128)}), f32[320,1920]{1,0:T(8,128)}) %reduce-scatter.27.cloned.1.call-update) | async-done | bytes 2457616 | tf_op jit(solution)/shard_map/reduce_scatter | solution.py:203
  1834.8 327.2 %reduce-scatter.25.cloned.1.call-done = f32[320,1920]{1,0:T(8,128)} async-done(((f32[2560,1920]{1,0:T(8,128)}), f32[320,1920]{1,0:T(8,128)}) %reduce-scatter.25.cloned.1.call-update) | async-done | bytes 2457616 | tf_op jit(solution)/shard_map/reduce_scatter | solution.py:202
  (502 shorter events, 331.2 us)
Async XLA Ops:
  7.2 168.8 %copy-start = (bf16[2560,640]{1,0:T(8,128)(2,1)S(1)}, bf16[2560,640]{1,0:T(8,128)(2,1)}, u32[]{:S(2)}) copy-start(bf16[2560,640]{1,0:T(8,128)(2,1)} %param.22) | copy-start | bytes 9830404
  7.2 217.2 %all-reduce.68.cloned.1.call-start = ((), (), s32[]{:S(2)}) async-start(), calls=%async_computation.10 | async-start | bytes 3276800 | tf_op jit(solution)/shard_map/psum | solution.py:118
  8.8 167.2 %copy-start.59 = (f32[160]{0:T(256)}, f32[160]{0:T(256)S(1)}, u32[]{:S(2)}) copy-start(f32[160]{0:T(256)S(1)} %add_rsqrt_fusion.1) | copy-start | bytes 1924
  12.6 8.1 collective-permute-start
  18.2 13.4 copy-start.56
  21.0 10.5 copy-start.21
  106.9 69.2 %copy-start.50 = (f32[2560]{0:T(1024)S(1)}, f32[2560]{0:T(1024)}, u32[]{:S(2)}) copy-start(f32[2560]{0:T(1024)} %param.20) | copy-start | bytes 30724
  181.7 45.9 %copy-start.55 = (f32[2560]{0:T(1024)S(1)}, f32[2560]{0:T(1024)}, u32[]{:S(2)}) copy-start(f32[2560]{0:T(1024)} %param.29) | copy-start | bytes 30724
  181.7 118.7 %all-reduce.70.cloned.1.call-start = ((), (), s32[]{:S(2)}) async-start(), calls=%async_computation.11 | async-start | bytes 3276800 | tf_op jit(solution)/shard_map/psum | solution.py:135
  256.2 274.9 %reduce-scatter.13.cloned.1.call-start = ((), (), s32[]{:S(2)}) async-start(), calls=%async_computation.12 | async-start | bytes 2048000 | tf_op jit(solution)/shard_map/reduce_scatter | solution.py:165
  433.8 42.9 %copy-start.58 = (f32[1,640]{1,0:T(1,128)S(1)}, f32[1,640]{1,0:T(1,128)}, u32[]{:S(2)}) copy-start(f32[1,640]{1,0:T(1,128)} %custom-call.1) | copy-start | bytes 7684
  481.5 12.6 copy-start.54
  481.5 12.6 copy-start.57
  481.5 12.6 copy-start.76
  502.7 108.0 %reduce-scatter.31.cloned.1.call-start = ((), (), s32[]{:S(2)}) async-start(), calls=%async_computation.21 | async-start | bytes 368640
  502.8 28.4 %copy-start.65 = (f32[1,3,640]{2,1,0:T(4,128)S(1)}, f32[1,3,640]{2,1,0:T(4,128)}, u32[]{:S(2)}) copy-start(f32[1,3,640]{2,1,0:T(4,128)} %copy-done.64) | copy-start | bytes 23044
  509.8 30.8 %copy-start.67 = (f32[640]{0:T(1024)S(1)}, f32[640]{0:T(1024)}, u32[]{:S(2)}) copy-start(f32[640]{0:T(1024)} %copy-done.66) | copy-start | bytes 7684
  509.8 30.8 %copy-start.69 = (f32[640]{0:T(1024)S(1)}, f32[640]{0:T(1024)}, u32[]{:S(2)}) copy-start(f32[640]{0:T(1024)} %copy-done.68) | copy-start | bytes 7684
  509.8 30.8 %copy-start.71 = (f32[640]{0:T(1024)S(1)}, f32[640]{0:T(1024)}, u32[]{:S(2)}) copy-start(f32[640]{0:T(1024)} %copy-done.70) | copy-start | bytes 7684
  509.8 30.8 %copy-start.73 = (f32[640]{0:T(1024)S(1)}, f32[640]{0:T(1024)}, u32[]{:S(2)}) copy-start(f32[640]{0:T(1024)} %copy-done.72) | copy-start | bytes 7684
  534.8 5.8 collective-permute-start.1
  537.1 135.4 %all-reduce.72.cloned.1.call-start = ((), (), s32[]{:S(2)}) async-start(), calls=%async_computation.22 | async-start | bytes 6553600 | tf_op jit(solution)/shard_map/psum | solution.py:125
  548.3 190.8 %reduce-scatter.21.cloned.1.call-start = ((), (), s32[]{:S(2)}) async-start(), calls=%async_computation.16 | async-start | bytes 737280 | tf_op jit(solution)/shard_map/reduce_scatter | solution.py:198
  557.2 247.5 %reduce-scatter.19.cloned.1.call-start = ((), (), s32[]{:S(2)}) async-start(), calls=%async_computation.15 | async-start | bytes 737280 | tf_op jit(solution)/shard_map/reduce_scatter | solution.py:197
  565.1 364.7 %reduce-scatter.23.cloned.1.call-start = ((), (), s32[]{:S(2)}) async-start(), calls=%async_computation.17 | async-start | bytes 7372800 | tf_op jit(solution)/shard_map/reduce_scatter | solution.py:200
  569.2 485.8 %reduce-scatter.17.cloned.1.call-start = ((), (), s32[]{:S(2)}) async-start(), calls=%async_computation.14 | async-start | bytes 7372800 | tf_op jit(solution)/shard_map/reduce_scatter | solution.py:194
  574.4 605.7 %reduce-scatter.15.cloned.1.call-start = ((), (), s32[]{:S(2)}) async-start(), calls=%async_computation.13 | async-start | bytes 7372800 | tf_op jit(solution)/shard_map/reduce_scatter | solution.py:193
  579.4 928.2 %reduce-scatter.29.cloned.1.call-start = ((), (), s32[]{:S(2)}) async-start(), calls=%async_computation.20 | async-start | bytes 22118400 | tf_op jit(solution)/shard_map/reduce_scatter | solution.py:204
  589.1 1245.7 %reduce-scatter.27.cloned.1.call-start = ((), (), s32[]{:S(2)}) async-start(), calls=%async_computation.19 | async-start | bytes 22118400 | tf_op jit(solution)/shard_map/reduce_scatter | solution.py:203
  598.6 1563.4 %reduce-scatter.25.cloned.1.call-start = ((), (), s32[]{:S(2)}) async-start(), calls=%async_computation.18 | async-start | bytes 22118400 | tf_op jit(solution)/shard_map/reduce_scatter | solution.py:202
  608.1 66.3 %copy-start.63 = (f32[2560]{0:T(1024)S(1)}, f32[2560]{0:T(1024)}, u32[]{:S(2)}) copy-start(f32[2560]{0:T(1024)} %get-tuple-element.241) | copy-start | bytes 30724
  714.3 1447.8 %copy-start.1 = (bf16[2560,640]{1,0:T(8,128)(2,1)S(1)}, bf16[2560,640]{1,0:T(8,128)(2,1)}, u32[]{:S(2)}) copy-start(bf16[2560,640]{1,0:T(8,128)(2,1)} %param.22) | copy-start | bytes 9830404
  (70 other events, 214.2 us)
Sparse Core Ops, SparseCore 0:
  181.8 42.5 all-reduce.67
  256.4 43.9 all-reduce.69
  502.8 28.2 reduce-scatter.12
  537.2 63.3 reduce-scatter.30
  602.8 69.6 all-reduce.71
  676.2 62.8 reduce-scatter.20
  743.0 61.7 reduce-scatter.18
  808.9 120.8 reduce-scatter.22
  934.0 120.9 reduce-scatter.16
  1059.0 120.9 reduce-scatter.14
  1184.6 323.0 reduce-scatter.28
  1512.0 322.7 reduce-scatter.26
  1839.3 322.7 reduce-scatter.24
where the time goes:
time: 2180 us; the launch traced here: 2170 us
  waiting for transfers between devices  1600 us (73%)
  local copies, waits for them, and re-layouts  193 us (9%)
  blocking collectives  138 us (6%)
  other arithmetic  115 us (5%)
  matrix products  101 us (5%)
    reduce_scatter x1, waiting for transfers between devices, per_device(): lax.psum_scatter(g_down, 'seq', scatter_dimension=1, tiled=True)  328 us
    reduce_scatter x1, waiting for transfers between devices, per_device(): lax.psum_scatter(g_gate, 'seq', scatter_dimension=0, tiled=True)  327 us
    reduce_scatter x1, waiting for transfers between devices, per_device(): lax.psum_scatter(g_up, 'seq', scatter_dimension=0, tiled=True)  327 us
    reduce_scatter x1, waiting for transfers between devices, per_device(): lax.psum_scatter(g_y, 'seq', scatter_dimension=0, tiled=True)  125 us
    reduce_scatter x1, waiting for transfers between devices, per_device(): lax.psum_scatter(g_x, 'seq', scatter_dimension=0, tiled=True)  125 us
    reduce_scatter x1, waiting for transfers between devices, per_device(): lax.psum_scatter(g_out, 'seq', scatter_dimension=1, tiled=True)  125 us
    dot_general x24, matrix products, bdot(): return jnp.dot(left, right, preferred_element_type=jnp.float32)  101 us
    all_gather x3, blocking collectives, carried_in(): pieces = jax.tree.map(lambda part: lax.all_gather(part, axis), value)  91.7 us
  transfers between devices with their start and end apart: 15, of which 13 were waited for; matrix products, arithmetic and copies ran while one was open for 5% of the time, Pallas kernels for 0%

commit v1 on v0

--- a/solution.py
+++ b/solution.py
@@ -122,7 +122,7 @@
     gate_pre = bdot(normed2, gate_weight)
     up_pre = bdot(normed2, up_weight)
     act = (gelu_tanh(gate_pre) * up_pre).astype(jnp.bfloat16)
-    ffn_out = lax.psum(bdot(act, down_weight), "mp")
+    ffn_out = jnp.sum(lax.all_gather(bdot(act, down_weight), "mp"), axis=0)
     block_output = (x_one + ffn_out).astype(jnp.bfloat16).reshape(seq_count, group_len, model_width)
     cot_low = out_cotangent.reshape(row_count, model_width)
     cot = cot_low.astype(jnp.float32)

time: 2180 us -> 2270 us (1.041)
  local copies, waits for them, and re-layouts: 193 us -> 240 us
    all_gather x0 -> x1, waiting for transfers between devices: none -> 47 us  [per_device(): ffn_out = jnp.sum(lax.all_gather(bdot(act, down_weight), 'mp'), axis=0)]
    reduce_scatter x1, waiting for transfers between devices: 20.2 us -> 65.6 us  [per_device(): lax.psum_scatter(g_decay_gate, 'seq', scatter_dimension=0, tiled=True)]
    reduce_scatter x1, waiting for transfers between devices: 65.6 us -> 21.1 us  [per_device(): lax.psum_scatter(g_input_gate, 'seq', scatter_dimension=0, tiled=True)]
    slice x48, local copies, waits for them, and re-layouts: 27.7 us -> 62.4 us  [per_device(): lax.associative_scan(link_pairs, (decay_three, drive.reshape(seq_count, g...]
    psum x1, waiting for transfers between devices: 60.4 us -> 33.6 us  [per_device(): lax.psum(bdot(d_x_branch, x_weight.T) + bdot(d_y_low, y_weight.T), 'mp')]
  transfers between devices with their start and end apart: 15 -> 16, of which waited for: 13 -> 14; matrix products, arithmetic and copies ran while one was open for 5% -> 4% of each run, Pallas kernels for 0% -> 0%
where the time goes in v1:
time: 2270 us; the launch traced here: 2250 us
  waiting for transfers between devices  1620 us (71%)
  local copies, waits for them, and re-layouts  240 us (11%)
  blocking collectives  138 us (6%)
  other arithmetic  132 us (6%)
  matrix products  101 us (4%)
    reduce_scatter x1, waiting for transfers between devices, per_device(): lax.psum_scatter(g_gate, 'seq', scatter_dimension=0, tiled=True)  327 us
    reduce_scatter x1, waiting for transfers between devices, per_device(): lax.psum_scatter(g_up, 'seq', scatter_dimension=0, tiled=True)  327 us
    reduce_scatter x1, waiting for transfers between devices, per_device(): lax.psum_scatter(g_down, 'seq', scatter_dimension=1, tiled=True)  327 us
    reduce_scatter x1, waiting for transfers between devices, per_device(): lax.psum_scatter(g_x, 'seq', scatter_dimension=0, tiled=True)  125 us
    reduce_scatter x1, waiting for transfers between devices, per_device(): lax.psum_scatter(g_y, 'seq', scatter_dimension=0, tiled=True)  125 us
    reduce_scatter x1, waiting for transfers between devices, per_device(): lax.psum_scatter(g_out, 'seq', scatter_dimension=1, tiled=True)  125 us
    dot_general x24, matrix products, bdot(): return jnp.dot(left, right, preferred_element_type=jnp.float32)  101 us
    all_gather x3, blocking collectives, carried_in(): pieces = jax.tree.map(lambda part: lax.all_gather(part, axis), value)  91.7 us
  transfers between devices with their start and end apart: 16, of which 14 were waited for; matrix products, arithmetic and copies ran while one was open for 4% of the time, Pallas kernels for 0%

profile of v1, /device:TPU:0, one launch (start us, length us, event | category | flops | bytes accessed | tf_op | source)
XLA Modules:
  0.0 2254.9 jit_solution(7385648948670464965)
XLA Ops:
  12.6 4.9 collective-permute-start
  21.1 8.8 all_gather.20
  150.5 30.8 %all_gather.22 = f32[8,1,640]{2,1,0:T(1,128)S(1)} all-gather(f32[1,1,640]{2,1,0:T(1,128)S(1)} %slice_add_fusion.1), channel_id=1, replica_groups=mesh['seq'=8,'mp'=4] {'seq'}, dimensions={0}, use_global_device_ids=true | all-gather | bytes 23040 | tf_op jit(solution)/shard_map/all_gather | solution.py:17
  187.7 30.4 %all_gather.21 = f32[8,1,640]{2,1,0:T(1,128)S(1)} all-gather(f32[1,1,640]{2,1,0:T(1,128)S(1)} %slice_add_fusion.2), channel_id=1, replica_groups=mesh['seq'=8,'mp'=4] {'seq'}, dimensions={0}, use_global_device_ids=true | all-gather | bytes 23040 | tf_op jit(solution)/shard_map/all_gather | solution.py:17
  224.6 42.2 %all-reduce.67.cloned.1.call-done = f32[160,2560]{1,0:T(8,128)} async-done(((f32[160,2560]{1,0:T(8,128)}), f32[160,2560]{1,0:T(8,128)}) %all-reduce.67.cloned.1.call-update) | async-done | bytes 1638416 | tf_op jit(solution)/shard_map/psum | solution.py:118
  270.1 6.2 fusion.117
  278.7 8.8 multiply_convert_fusion.1
  290.9 8.3 convolution_add_fusion.2
  299.3 7.0 fusion.119
  323.2 20.2 all-reduce.69.cloned.1.call-done
  346.5 47.0 %all-gather.3.cloned.1.call-done = f32[640,2560]{1,0:T(8,128)} async-done(((f32[160,2560]{1,0:T(8,128)}), f32[640,2560]{1,0:T(8,128)}) %all-gather.3.cloned.1.call-update) | async-done | bytes 6553616 | tf_op jit(solution)/shard_map/all_gather | solution.py:125
  393.5 4.7 reduce_sum.137
  398.2 4.4 multiply_add_fusion
  404.7 5.6 reverse.8
  551.5 30.5 %all_gather.25 = f32[8,1,640]{2,1,0:T(1,128)S(1)} all-gather(f32[1,1,640]{2,1,0:T(1,128)S(1)} %add_multiply_fusion.20), channel_id=1, replica_groups=mesh['seq'=8,'mp'=4] {'seq'}, dimensions={0}, use_global_device_ids=true | all-gather | bytes 23040 | tf_op jit(solution)/shard_map/all_gather | solution.py:17
  582.0 4.8 while.29
  595.4 5.6 rev.18
  601.0 5.6 rev.17
  615.3 28.3 %reduce-scatter.13.cloned.1.call-done = f32[160,640]{1,0:T(8,128)} async-done(((f32[160,2560]{1,0:T(8,128)}), f32[160,640]{1,0:T(8,128)}) %reduce-scatter.13.cloned.1.call-update) | async-done | bytes 409616 | tf_op jit(solution)/shard_map/reduce_scatter | solution.py:165
  693.3 8.2 fusion.122
  702.5 8.2 fusion.123
  712.1 8.6 fusion.36
  724.7 33.6 %all-reduce.71.cloned.1.call-done = f32[160,2560]{1,0:T(8,128)} async-done(((f32[160,2560]{1,0:T(8,128)}), f32[160,2560]{1,0:T(8,128)}) %all-reduce.71.cloned.1.call-update) | async-done | bytes 1638416 | tf_op jit(solution)/shard_map/psum | solution.py:186
  760.3 37.4 %all-reduce.62 = (f32[2560]{0:T(1024)S(1)}, f32[640]{0:T(1024)S(1)}, f32[640]{0:T(1024)S(1)}, f32[2560]{0:T(1024)S(1)}) all-reduce(f32[2560]{0:T(1024)S(1)} %get-tuple-element.243, f32[640]{0:T(1024)S(1)} %get-tuple-element.248, f32[640]{0:T(1024)S(1)} %get-tuple-element.279, ...), channel_id=4, replica_groups=mesh['seq'=8,'mp'=4] {'seq'}, use_global_device_ids=true, to_apply=%region_14.15.clone | all-reduce | flops 6400 | bytes 51200
  804.0 21.1 reduce-scatter.19.cloned.1.call-done
  825.1 65.6 %reduce-scatter.21.cloned.1.call-done = f32[32,640]{1,0:T(8,128)} async-done(((f32[256,640]{1,0:T(8,128)}), f32[32,640]{1,0:T(8,128)}) %reduce-scatter.21.cloned.1.call-update) | async-done | bytes 81936 | tf_op jit(solution)/shard_map/reduce_scatter | solution.py:198
  890.7 125.0 %reduce-scatter.23.cloned.1.call-done = f32[640,320]{0,1:T(8,128)} async-done(((f32[640,2560]{0,1:T(8,128)}), f32[640,320]{0,1:T(8,128)}) %reduce-scatter.23.cloned.1.call-update) | async-done | bytes 819216 | tf_op jit(solution)/shard_map/reduce_scatter | solution.py:200
  1015.7 125.1 %reduce-scatter.17.cloned.1.call-done = f32[320,640]{1,0:T(8,128)} async-done(((f32[2560,640]{1,0:T(8,128)}), f32[320,640]{1,0:T(8,128)}) %reduce-scatter.17.cloned.1.call-update) | async-done | bytes 819216 | tf_op jit(solution)/shard_map/reduce_scatter | solution.py:194
  1140.8 125.2 %reduce-scatter.15.cloned.1.call-done = f32[320,640]{1,0:T(8,128)} async-done(((f32[2560,640]{1,0:T(8,128)}), f32[320,640]{1,0:T(8,128)}) %reduce-scatter.15.cloned.1.call-update) | async-done | bytes 819216 | tf_op jit(solution)/shard_map/reduce_scatter | solution.py:193
  1266.0 327.5 %reduce-scatter.25.cloned.1.call-done = f32[320,1920]{1,0:T(8,128)} async-done(((f32[2560,1920]{1,0:T(8,128)}), f32[320,1920]{1,0:T(8,128)}) %reduce-scatter.25.cloned.1.call-update) | async-done | bytes 2457616 | tf_op jit(solution)/shard_map/reduce_scatter | solution.py:202
  1593.4 327.4 %reduce-scatter.27.cloned.1.call-done = f32[320,1920]{1,0:T(8,128)} async-done(((f32[2560,1920]{1,0:T(8,128)}), f32[320,1920]{1,0:T(8,128)}) %reduce-scatter.27.cloned.1.call-update) | async-done | bytes 2457616 | tf_op jit(solution)/shard_map/reduce_scatter | solution.py:203
  1920.9 327.3 %reduce-scatter.29.cloned.1.call-done = f32[1920,320]{0,1:T(8,128)} async-done(((f32[1920,2560]{0,1:T(8,128)}), f32[1920,320]{0,1:T(8,128)}) %reduce-scatter.29.cloned.1.call-update) | async-done | bytes 2457616 | tf_op jit(solution)/shard_map/reduce_scatter | solution.py:204
  (498 shorter events, 398.7 us)
Async XLA Ops:
  7.2 211.3 %copy-start = (bf16[2560,640]{1,0:T(8,128)(2,1)S(1)}, bf16[2560,640]{1,0:T(8,128)(2,1)}, u32[]{:S(2)}) copy-start(bf16[2560,640]{1,0:T(8,128)(2,1)} %param.22) | copy-start | bytes 9830404
  7.2 259.6 %all-reduce.67.cloned.1.call-start = ((), (), s32[]{:S(2)}) async-start(), calls=%async_computation.10 | async-start | bytes 3276800 | tf_op jit(solution)/shard_map/psum | solution.py:118
  8.8 209.6 %copy-start.51 = (f32[160]{0:T(256)}, f32[160]{0:T(256)S(1)}, u32[]{:S(2)}) copy-start(f32[160]{0:T(256)S(1)} %add_rsqrt_fusion.1) | copy-start | bytes 1924
  12.6 8.1 collective-permute-start
  88.0 18.3 copy-start.56
  88.0 22.4 copy-start.43
  144.1 37.2 %copy-start.35 = (f32[1,79,640]{2,1,0:T(8,128)S(1)}, f32[1,79,640]{2,1,0:T(8,128)}, u32[]{:S(2)}) copy-start(f32[1,79,640]{2,1,0:T(8,128)} %get-tuple-element.304) | copy-start | bytes 606724
  144.8 73.7 %copy-start.42 = (f32[2560]{0:T(1024)S(1)}, f32[2560]{0:T(1024)}, u32[]{:S(2)}) copy-start(f32[2560]{0:T(1024)} %param.20) | copy-start | bytes 30724
  224.0 45.9 %copy-start.47 = (f32[2560]{0:T(1024)S(1)}, f32[2560]{0:T(1024)}, u32[]{:S(2)}) copy-start(f32[2560]{0:T(1024)} %param.29) | copy-start | bytes 30724
  224.0 119.4 %all-reduce.69.cloned.1.call-start = ((), (), s32[]{:S(2)}) async-start(), calls=%async_computation.11 | async-start | bytes 3276800 | tf_op jit(solution)/shard_map/psum | solution.py:135
  299.3 94.2 %all-gather.3.cloned.1.call-start = ((), (), s32[]{:S(2)}) async-start(), calls=%async_computation.22 | async-start | bytes 8192000 | tf_op jit(solution)/shard_map/all_gather | solution.py:125
  306.4 337.3 %reduce-scatter.13.cloned.1.call-start = ((), (), s32[]{:S(2)}) async-start(), calls=%async_computation.12 | async-start | bytes 2048000 | tf_op jit(solution)/shard_map/reduce_scatter | solution.py:165
  543.5 38.5 %copy-start.50 = (f32[1,640]{1,0:T(1,128)S(1)}, f32[1,640]{1,0:T(1,128)}, u32[]{:S(2)}) copy-start(f32[1,640]{1,0:T(1,128)} %custom-call.1) | copy-start | bytes 7684
  591.0 15.6 copy-start.69
  615.2 28.5 %copy-start.58 = (f32[1,3,640]{2,1,0:T(4,128)S(1)}, f32[1,3,640]{2,1,0:T(4,128)}, u32[]{:S(2)}) copy-start(f32[1,3,640]{2,1,0:T(4,128)} %copy-done.57) | copy-start | bytes 23044
  615.2 37.9 %copy-start.60 = (f32[640]{0:T(1024)S(1)}, f32[640]{0:T(1024)}, u32[]{:S(2)}) copy-start(f32[640]{0:T(1024)} %copy-done.59) | copy-start | bytes 7684
  615.2 37.9 %copy-start.62 = (f32[640]{0:T(1024)S(1)}, f32[640]{0:T(1024)}, u32[]{:S(2)}) copy-start(f32[640]{0:T(1024)} %copy-done.61) | copy-start | bytes 7684
  615.2 37.9 %copy-start.64 = (f32[640]{0:T(1024)S(1)}, f32[640]{0:T(1024)}, u32[]{:S(2)}) copy-start(f32[640]{0:T(1024)} %copy-done.63) | copy-start | bytes 7684
  615.2 37.9 %copy-start.66 = (f32[640]{0:T(1024)S(1)}, f32[640]{0:T(1024)}, u32[]{:S(2)}) copy-start(f32[640]{0:T(1024)} %copy-done.65) | copy-start | bytes 7684
  615.3 108.0 %reduce-scatter.31.cloned.1.call-start = ((), (), s32[]{:S(2)}) async-start(), calls=%async_computation.23 | async-start | bytes 368640
  647.4 5.8 collective-permute-start.1
  649.6 108.7 %all-reduce.71.cloned.1.call-start = ((), (), s32[]{:S(2)}) async-start(), calls=%async_computation.13 | async-start | bytes 3276800 | tf_op jit(solution)/shard_map/psum | solution.py:186
  660.8 164.3 %reduce-scatter.19.cloned.1.call-start = ((), (), s32[]{:S(2)}) async-start(), calls=%async_computation.16 | async-start | bytes 737280 | tf_op jit(solution)/shard_map/reduce_scatter | solution.py:197
  669.8 220.9 %reduce-scatter.21.cloned.1.call-start = ((), (), s32[]{:S(2)}) async-start(), calls=%async_computation.17 | async-start | bytes 737280 | tf_op jit(solution)/shard_map/reduce_scatter | solution.py:198
  677.7 338.1 %reduce-scatter.23.cloned.1.call-start = ((), (), s32[]{:S(2)}) async-start(), calls=%async_computation.18 | async-start | bytes 7372800 | tf_op jit(solution)/shard_map/reduce_scatter | solution.py:200
  681.7 459.0 %reduce-scatter.17.cloned.1.call-start = ((), (), s32[]{:S(2)}) async-start(), calls=%async_computation.15 | async-start | bytes 7372800 | tf_op jit(solution)/shard_map/reduce_scatter | solution.py:194
  687.0 579.0 %reduce-scatter.15.cloned.1.call-start = ((), (), s32[]{:S(2)}) async-start(), calls=%async_computation.14 | async-start | bytes 7372800 | tf_op jit(solution)/shard_map/reduce_scatter | solution.py:193
  692.0 901.5 %reduce-scatter.25.cloned.1.call-start = ((), (), s32[]{:S(2)}) async-start(), calls=%async_computation.19 | async-start | bytes 22118400 | tf_op jit(solution)/shard_map/reduce_scatter | solution.py:202
  701.5 1219.4 %reduce-scatter.27.cloned.1.call-start = ((), (), s32[]{:S(2)}) async-start(), calls=%async_computation.20 | async-start | bytes 22118400 | tf_op jit(solution)/shard_map/reduce_scatter | solution.py:203
  710.8 1537.4 %reduce-scatter.29.cloned.1.call-start = ((), (), s32[]{:S(2)}) async-start(), calls=%async_computation.21 | async-start | bytes 22118400 | tf_op jit(solution)/shard_map/reduce_scatter | solution.py:204
  720.7 39.6 %copy-start.55 = (f32[2560]{0:T(1024)S(1)}, f32[2560]{0:T(1024)}, u32[]{:S(2)}) copy-start(f32[2560]{0:T(1024)} %get-tuple-element.241) | copy-start | bytes 30724
  800.2 1447.9 %copy-start.1 = (bf16[2560,640]{1,0:T(8,128)(2,1)S(1)}, bf16[2560,640]{1,0:T(8,128)(2,1)}, u32[]{:S(2)}) copy-start(bf16[2560,640]{1,0:T(8,128)(2,1)} %param.22) | copy-start | bytes 9830404
  (67 other events, 306.0 us)
Sparse Core Ops, SparseCore 0:
  224.1 42.5 all-reduce.66
  299.4 43.9 all-reduce.68
  345.6 47.8 all-gather.2
  615.3 28.2 reduce-scatter.12
  649.7 63.3 reduce-scatter.30
  715.3 42.9 all-reduce.70
  762.2 62.8 reduce-scatter.18
  829.0 61.6 reduce-scatter.20
  894.9 120.7 reduce-scatter.22
  1019.8 120.9 reduce-scatter.16
  1145.0 120.9 reduce-scatter.14
  1270.3 323.0 reduce-scatter.24
  1597.9 322.9 reduce-scatter.26
  1925.2 322.8 reduce-scatter.28
